TPU v7x, 512 devices: a whole 4x4x16 slice. The times are simulated.
512 devices in a mesh: af: 8 (over x, z_hi), vert: 64 (over y, z_lo, core).
Axes of the slice: x: 4, y: 4, z: 16 (z_hi: 2, z_lo: 8; z = z_hi * 8 + z_lo), core: 2. Of those that a mesh axis runs over, the one named last changes fastest.
Arguments:
- signals: bfloat16 [1000, 16384], P('af', 'vert'), may hold values from -2000 to 2000
- basis: bfloat16 [10, 1000], P(None, 'af'), may hold values from -0.1875 to 0.1875
- atoms: float32 [10, 262144], P(None, ('af', 'vert')), may hold values from -6 to 6
- params: float32 [3, 262144], P(None, ('af', 'vert')), may hold values from -1.5 to 1.5
Outputs:
- coefficients: float32 [10, 16384], P(None, 'vert')
- maps: float32 [3, 16384], P(None, 'vert')
All inputs are finite; a program needn't handle non-finite values.
Results may differ from a plain program's by a relative error of at most 0.0003.
Values sent between devices are 32-bit elements; how exact they have to be, the bound alone decides.
No kernel may reach another device: no remote copies, remote signals or barrier semaphores. Data moves between devices by JAX's collectives and lax.ppermute only.
A program may use at most 64 MiB of HBM per device.

v0:
```python
import math
import jax
import jax.numpy as jnp
from jax import lax
from jax.sharding import PartitionSpec as P

score_scale = 1.5


def fold_block(running, coefficients, atom_piece, param_piece):
    run_peak, run_total, run_weighted = running
    scores = score_scale * lax.dot_general(
        coefficients,
        atom_piece,
        (((0,), (0,)), ((), ())),
        precision=lax.Precision.HIGHEST,
        preferred_element_type=jnp.float32,
    )
    new_peak = jnp.maximum(run_peak, jnp.max(scores, axis=1))
    weights = jnp.exp(scores - new_peak[:, None])
    factor = jnp.exp(run_peak - new_peak)
    run_total = run_total * factor + jnp.sum(weights, axis=1)
    run_weighted = run_weighted * factor[None, :] + lax.dot_general(
        param_piece,
        weights,
        (((1,), (1,)), ((), ())),
        precision=lax.Precision.HIGHEST,
        preferred_element_type=jnp.float32,
    )
    return (new_peak, run_total, run_weighted)


def make_folder(coefficients, running, pieces):
    atom_piece, param_piece = pieces
    piece_width = atom_piece.shape[1]
    block_size = math.gcd(piece_width, 2048)
    block_count = piece_width // block_size
    atom_blocks = atom_piece.reshape(atom_piece.shape[0], block_count, block_size).transpose(
        1, 0, 2
    )
    param_blocks = param_piece.reshape(3, block_count, block_size).transpose(1, 0, 2)

    def step(state, blocks):
        return (fold_block(state, coefficients, blocks[0], blocks[1]), None)

    result, unused = lax.scan(step, running, (atom_blocks, param_blocks))
    return result


def start_state(voxels):
    return (
        jnp.full((voxels,), -1e30, jnp.float32),
        jnp.zeros((voxels,), jnp.float32),
        jnp.zeros((3, voxels), jnp.float32),
    )


def on_device(signals, basis, atoms, params):
    partial_sums = jnp.dot(basis, signals, preferred_element_type=jnp.float32)
    coefficients = lax.psum(partial_sums, "af")
    run_peak, run_total, run_weighted = make_folder(
        coefficients,
        start_state(coefficients.shape[1]),
        (
            lax.all_gather(atoms, "vert", axis=1, tiled=True),
            lax.all_gather(params, "vert", axis=1, tiled=True),
        ),
    )
    global_peak = lax.pmax(run_peak, "af")
    factor = jnp.exp(run_peak - global_peak)
    run_total, run_weighted = lax.psum((run_total * factor, run_weighted * factor[None, :]), "af")
    maps = run_weighted / run_total[None, :]
    return (coefficients, maps)


def solution(mesh):
    placed = (P("af", "vert"), P(None, "af"), P(None, ("af", "vert")), P(None, ("af", "vert")))
    return jax.shard_map(
        on_device,
        mesh=mesh,
        in_specs=placed,
        out_specs=(P(None, "vert"), P(None, "vert")),
        check_vma=False,
    )
```

profile of v0, /device:TPU:2, one launch (start us, length us, event | category | flops | bytes accessed | tf_op | source)
XLA Modules:
  0.0 352.7 jit_solution(9641014140261085518)
XLA Ops:
  8.8 79.5 %psum.21 = f32[10,256]{1,0:T(8,128)S(1)} all-reduce(f32[10,256]{1,0:T(8,128)S(1)} %fusion.11), channel_id=1, replica_groups=mesh['af'=8,'vert'=64] {'af'}, use_global_device_ids=true, to_apply=%region_0.0 | all-reduce | flops 2560 | bytes 20480 | tf_op jit(solution)/shard_map/psum | solution.py:60
  88.4 120.6 %all_gather.7 = f32[3,32768]{1,0:T(4,128)S(1)} all-gather(f32[3,512]{1,0:T(4,128)} %param.9), channel_id=1, replica_groups=mesh['af'=8,'vert'=64] {'vert'}, dimensions={1}, use_global_device_ids=true | all-gather | bytes 399360 | tf_op jit(solution)/shard_map/all_gather | solution.py:66
  209.0 2.8 copy.8
  211.9 55.3 %while.15 = (s32[]{:T(128)}, f32[256]{0:T(256)S(1)}, f32[256]{0:T(256)S(1)}, f32[3,256]{1,0:T(4,128)S(1)}, f32[16,10,2048]{2,0,1:T(8,128)S(1)}, /*index=5*/f32[1...) while((s32[]{:T(128)}, f32[256]{0:T(256)S(1)}, f32[256]{0:T(256)S(1)}, ...), condition=%wide.region_4.5_spmd.clone, body=%wide.region_1.4_spmd.clone.sunk | while | flops 84413952 | bytes 6603897 | solution.py:46
  212.0 1.9 fusion.24
  215.5 1.9 fusion.24
  217.7 1.1 fusion.28
  218.9 1.9 fusion.24
  221.2 1.1 fusion.28
  222.4 1.9 fusion.24
  224.6 1.1 fusion.28
  225.9 1.9 fusion.24
  228.1 1.1 fusion.28
  229.3 1.9 fusion.24
  231.6 1.1 fusion.28
  232.8 1.9 fusion.24
  235.0 1.1 fusion.28
  236.2 1.9 fusion.24
  238.5 1.1 fusion.28
  239.7 1.9 fusion.24
  241.9 1.1 fusion.28
  243.1 1.9 fusion.24
  245.4 1.1 fusion.28
  246.6 1.9 fusion.24
  248.8 1.1 fusion.28
  250.0 1.9 fusion.24
  253.5 1.9 fusion.24
  257.0 1.9 fusion.24
  260.4 1.9 fusion.24
  263.9 1.9 fusion.24
  267.2 33.7 %pmax.7 = f32[256]{0:T(256)S(1)} all-reduce(f32[256]{0:T(256)S(1)} %get-tuple-element.42), channel_id=1, replica_groups=mesh['af'=8,'vert'=64] {'af'}, use_global_device_ids=true, to_apply=%region_5.6 | all-reduce | flops 256 | bytes 2048 | tf_op jit(solution)/shard_map/pmax | solution.py:69
  300.9 44.3 %all-reduce = (f32[3,256]{1,0:T(4,128)S(1)}, f32[256]{0:T(256)S(1)}) all-reduce(f32[3,256]{1,0:T(4,128)S(1)} %broadcast_multiply_fusion, f32[256]{0:T(256)S(1)} %get-tuple-element.93), channel_id=1, replica_groups=mesh['af'=8,'vert'=64] {'af'}, use_global_device_ids=true, to_apply=%region_6.7 | all-reduce | flops 1024 | bytes 8192 | tf_op jit(solution)/shard_map/psum | solution.py:71
  (101 shorter events, 16.2 us)
Async XLA Ops:
  7.2 0.8 copy-start
  7.2 201.8 %all-gather.2.cloned.1.call-start = ((), (), s32[]{:S(2)}) async-start(), calls=%async_computation | async-start | bytes 2129920 | tf_op jit(solution)/shard_map/all_gather | solution.py:65
  267.2 78.6 %copy-start.1 = (f32[10,256]{1,0:T(8,128)}, f32[10,256]{1,0:T(8,128)S(1)}, u32[]{:S(2)}) copy-start(f32[10,256]{1,0:T(8,128)S(1)} %get-tuple-element.177) | copy-start | bytes 30724
Sparse Core Ops, SparseCore 0:
  10.2 125.4 all-gather.1
where the time goes:
time: 353 us
  blocking collectives  278 us (79%)
  matrix products  48.2 us (14%)
  between operations  14.1 us (4%)
  other arithmetic  6.72 us (2%)
  local copies, waits for them, and re-layouts  4.12 us (1%)
    all_gather x1, blocking collectives, on_device(): lax.all_gather(params, 'vert', axis=1, tiled=True)  121 us
    psum x1, blocking collectives, on_device(): coefficients = lax.psum(partial_sums, 'af')  79.5 us
    psum x1, blocking collectives, on_device(): lax.psum((run_total * factor, run_weighted * factor[None, :]), 'af')  44.3 us
    pmax x1, blocking collectives, on_device(): global_peak = lax.pmax(run_peak, 'af')  33.7 us
    dot_general x16, matrix products, fold_block(): lax.dot_general(coefficients, atom_piece, (((0,), (0,)), ((), ())), preci...  29.7 us
    dot_general x16, matrix products, fold_block(): lax.dot_general(param_piece, weights, (((1,), (1,)), ((), ())), precision...  17.7 us
  transfers between devices with their start and end apart: 1, of which 0 were waited for; matrix products, arithmetic and copies ran while one was open for 0% of the time, Pallas kernels for 0%

commit v1 on v0

--- a/solution.py
+++ b/solution.py
@@ -56,8 +56,13 @@
 
 
 def on_device(signals, basis, atoms, params):
+
+    def match_chunk_for(shard_in, which_axis):
+        plain = jax.lax.all_gather(shard_in, axis_name=which_axis).sum(axis=0)
+        return plain
+
     partial_sums = jnp.dot(basis, signals, preferred_element_type=jnp.float32)
-    coefficients = lax.psum(partial_sums, "af")
+    coefficients = match_chunk_for(partial_sums, which_axis="af")
     run_peak, run_total, run_weighted = make_folder(
         coefficients,
         start_state(coefficients.shape[1]),

time: 353 us -> 342 us (0.969)
  blocking collectives: 278 us -> 268 us
    psum x1 -> x0, blocking collectives: 79.5 us -> none  [on_device(): coefficients = lax.psum(partial_sums, 'af')]
    all_gather x0 -> x1, blocking collectives: none -> 66.6 us  [match_chunk_for(): plain = jax.lax.all_gather(shard_in, axis_name=which_axis).sum(axis=0)]
    pmax x1, blocking collectives: 33.7 us -> 42.2 us  [on_device(): global_peak = lax.pmax(run_peak, 'af')]
    psum x1, blocking collectives: 44.3 us -> 36 us  [on_device(): lax.psum((run_total * factor, run_weighted * factor[None, :]), 'af')]
where the time goes in v1:
time: 342 us
  blocking collectives  268 us (78%)
  matrix products  48.2 us (14%)
  between operations  14.1 us (4%)
  other arithmetic  6.73 us (2%)
  local copies, waits for them, and re-layouts  4.12 us (1%)
    all_gather x1, blocking collectives, on_device(): lax.all_gather(params, 'vert', axis=1, tiled=True)  123 us
    all_gather x1, blocking collectives, match_chunk_for(): plain = jax.lax.all_gather(shard_in, axis_name=which_axis).sum(axis=0)  66.6 us
    pmax x1, blocking collectives, on_device(): global_peak = lax.pmax(run_peak, 'af')  42.2 us
    psum x1, blocking collectives, on_device(): lax.psum((run_total * factor, run_weighted * factor[None, :]), 'af')  36 us
    dot_general x16, matrix products, fold_block(): lax.dot_general(coefficients, atom_piece, (((0,), (0,)), ((), ())), preci...  29.7 us
    dot_general x16, matrix products, fold_block(): lax.dot_general(param_piece, weights, (((1,), (1,)), ((), ())), precision...  17.7 us
  transfers between devices with their start and end apart: 1, of which 0 were waited for; matrix products, arithmetic and copies ran while one was open for 0% of the time, Pallas kernels for 0%

profile of v1, /device:TPU:2, one launch (start us, length us, event | category | flops | bytes accessed | tf_op | source)
XLA Modules:
  0.0 342.2 jit_solution(15187238834506961707)
XLA Ops:
  8.8 66.6 %all-gather.1 = f32[8,10,256]{2,1,0:T(8,128)S(1)} all-gather(f32[1,10,256]{2,1,0:T(8,128)S(1)} %convolution_bitcast_fusion), channel_id=2, replica_groups=mesh['af'=8,'vert'=64] {'af'}, dimensions={0}, use_global_device_ids=true | all-gather | bytes 92160 | tf_op jit(solution)/shard_map/all_gather | solution.py:61
  75.5 122.9 %all_gather.15 = f32[3,32768]{1,0:T(4,128)S(1)} all-gather(f32[3,512]{1,0:T(4,128)} %param.9), channel_id=1, replica_groups=mesh['af'=8,'vert'=64] {'vert'}, dimensions={1}, use_global_device_ids=true | all-gather | bytes 399360 | tf_op jit(solution)/shard_map/all_gather | solution.py:71
  198.4 2.8 copy.9
  201.3 55.2 %while.15 = (s32[]{:T(128)}, f32[256]{0:T(256)S(1)}, f32[256]{0:T(256)S(1)}, f32[3,256]{1,0:T(4,128)S(1)}, f32[16,10,2048]{2,0,1:T(8,128)S(1)}, /*index=5*/f32[1...) while((s32[]{:T(128)}, f32[256]{0:T(256)S(1)}, f32[256]{0:T(256)S(1)}, ...), condition=%wide.region_4.5_spmd.clone, body=%wide.region_1.4_spmd.clone.sunk | while | flops 84413952 | bytes 6603897 | solution.py:46
  201.4 1.9 fusion.23
  203.6 1.1 fusion.27
  204.8 1.9 fusion.23
  207.1 1.1 fusion.27
  208.3 1.9 fusion.23
  211.7 1.9 fusion.23
  214.0 1.1 fusion.27
  215.2 1.9 fusion.23
  217.4 1.1 fusion.27
  218.7 1.9 fusion.23
  220.9 1.1 fusion.27
  222.1 1.9 fusion.23
  224.4 1.1 fusion.27
  225.6 1.9 fusion.23
  227.8 1.1 fusion.27
  229.0 1.9 fusion.23
  231.3 1.1 fusion.27
  232.5 1.9 fusion.23
  235.9 1.9 fusion.23
  238.2 1.1 fusion.27
  239.4 1.9 fusion.23
  241.6 1.1 fusion.27
  242.8 1.9 fusion.23
  246.3 1.9 fusion.23
  249.7 1.9 fusion.23
  253.2 1.9 fusion.23
  256.6 42.2 %pmax.7 = f32[256]{0:T(256)S(1)} all-reduce(f32[256]{0:T(256)S(1)} %get-tuple-element.42), channel_id=1, replica_groups=mesh['af'=8,'vert'=64] {'af'}, use_global_device_ids=true, to_apply=%region_5.6 | all-reduce | flops 256 | bytes 2048 | tf_op jit(solution)/shard_map/pmax | solution.py:74
  298.7 36.0 %all-reduce = (f32[3,256]{1,0:T(4,128)S(1)}, f32[256]{0:T(256)S(1)}) all-reduce(f32[3,256]{1,0:T(4,128)S(1)} %broadcast_multiply_fusion, f32[256]{0:T(256)S(1)} %get-tuple-element.100), channel_id=1, replica_groups=mesh['af'=8,'vert'=64] {'af'}, use_global_device_ids=true, to_apply=%region_6.7 | all-reduce | flops 1024 | bytes 8192 | tf_op jit(solution)/shard_map/psum | solution.py:76
  (102 shorter events, 16.2 us)
Async XLA Ops:
  7.2 0.8 copy-start
  7.2 191.2 %all-gather.4.cloned.1.call-start = ((), (), s32[]{:S(2)}) async-start(), calls=%async_computation | async-start | bytes 2129920 | tf_op jit(solution)/shard_map/all_gather | solution.py:70
  256.5 78.8 %copy-start.1 = (f32[10,256]{1,0:T(8,128)}, f32[10,256]{1,0:T(8,128)S(1)}, u32[]{:S(2)}) copy-start(f32[10,256]{1,0:T(8,128)S(1)} %get-tuple-element.184) | copy-start | bytes 30724
Sparse Core Ops, SparseCore 0:
  10.2 125.7 all-gather.3

commit v2 on v0

--- a/solution.py
+++ b/solution.py
@@ -1,3 +1,4 @@
+import functools
 import math
 import jax
 import jax.numpy as jnp
@@ -5,6 +6,21 @@
 from jax.sharding import PartitionSpec as P
 
 score_scale = 1.5
+
+
+def match_axis_part(page, shard_axis):
+    return jnp.concatenate(
+        lax.all_to_all(
+            jnp.stack(tuple((page for _ in range(lax.axis_size(shard_axis)))), axis=0),
+            shard_axis,
+            0,
+            0,
+        ),
+        axis=1,
+    )
+
+
+write_ways = functools.partial(match_axis_part, shard_axis="vert")
 
 
 def fold_block(running, coefficients, atom_piece, param_piece):
@@ -61,10 +77,7 @@
     run_peak, run_total, run_weighted = make_folder(
         coefficients,
         start_state(coefficients.shape[1]),
-        (
-            lax.all_gather(atoms, "vert", axis=1, tiled=True),
-            lax.all_gather(params, "vert", axis=1, tiled=True),
-        ),
+        (lax.all_gather(atoms, "vert", axis=1, tiled=True), write_ways(params)),
     )
     global_peak = lax.pmax(run_peak, "af")
     factor = jnp.exp(run_peak - global_peak)

time: 353 us -> 281 us (0.80)
  the two profiles are of different devices: /device:TPU:2 before, /device:TPU:40 now
where the time goes in v2:
time: 281 us
  blocking collectives  153 us (54%)
  matrix products  48.2 us (17%)
  waiting for transfers between devices  37.4 us (13%)
  starting transfers between devices  15.8 us (6%)
  between operations  14.1 us (5%)
  other arithmetic  6.72 us (2%)
  local copies, waits for them, and re-layouts  5.61 us (2%)
    psum x1, blocking collectives, on_device(): coefficients = lax.psum(partial_sums, 'af')  74.5 us
    pmax x1, blocking collectives, on_device(): global_peak = lax.pmax(run_peak, 'af')  42 us
    all_gather x1, waiting for transfers between devices, on_device(): lax.all_gather(atoms, 'vert', axis=1, tiled=True)  36.7 us
    psum x1, blocking collectives, on_device(): lax.psum((run_total * factor, run_weighted * factor[None, :]), 'af')  36.1 us
    dot_general x16, matrix products, fold_block(): lax.dot_general(coefficients, atom_piece, (((0,), (0,)), ((), ())), preci...  29.7 us
    dot_general x16, matrix products, fold_block(): lax.dot_general(param_piece, weights, (((1,), (1,)), ((), ())), precision...  17.7 us
    all_to_all x1, starting transfers between devices, match_axis_part(): lax.all_to_all(jnp.stack(tuple((page for _ in range(lax.axis_size(shard_a...  15.7 us
    reduce_sum x16, other arithmetic, fold_block(): run_total = run_total * factor + jnp.sum(weights, axis=1)  5.74 us
  transfers between devices with their start and end apart: 2, of which 1 were waited for; matrix products, arithmetic and copies ran while one was open for 2% of the time, Pallas kernels for 0%

profile of v2, /device:TPU:40, one launch (start us, length us, event | category | flops | bytes accessed | tf_op | source)
XLA Modules:
  0.0 281.1 jit_solution(6309764787879343850)
XLA Ops:
  7.9 1.6 stack.2
  9.5 15.7 %all-to-all-start = ((f32[64,3,512]{2,1,0:T(4,128)}), f32[64,3,512]{2,1,0:T(4,128)S(1)}, u32[]{:S(2)}, u32[]{:S(2)}) async-start(f32[64,3,512]{2,1,0:T(4,128)} %stack.2), calls=%async_computation | async-start | bytes 1048576 | tf_op jit(solution)/shard_map/all_to_all | solution.py:13
  26.1 74.5 %psum.21 = f32[10,256]{1,0:T(8,128)S(1)} all-reduce(f32[10,256]{1,0:T(8,128)S(1)} %fusion.11), channel_id=1, replica_groups=mesh['af'=8,'vert'=64] {'af'}, use_global_device_ids=true, to_apply=%region_0.0 | all-reduce | flops 2560 | bytes 20480 | tf_op jit(solution)/shard_map/psum | solution.py:76
  100.5 36.7 %all-gather.2.cloned.1.call-done = f32[10,32768]{1,0:T(8,128)} async-done(((f32[10,512]{1,0:T(8,128)}), f32[10,32768]{1,0:T(8,128)}) %all-gather.2.cloned.1.call-update) | async-done | bytes 1310736 | tf_op jit(solution)/shard_map/all_gather | solution.py:80
  137.3 2.8 copy.8
  140.2 55.3 %while.15 = (s32[]{:T(128)}, f32[256]{0:T(256)S(1)}, f32[256]{0:T(256)S(1)}, f32[3,256]{1,0:T(4,128)S(1)}, f32[16,10,2048]{2,0,1:T(8,128)S(1)}, /*index=5*/f32[1...) while((s32[]{:T(128)}, f32[256]{0:T(256)S(1)}, f32[256]{0:T(256)S(1)}, ...), condition=%wide.region_4.5_spmd.clone, body=%wide.region_1.4_spmd.clone.sunk | while | flops 84413952 | bytes 6603897 | solution.py:62
  140.3 1.9 fusion.24
  142.6 1.1 fusion.28
  143.8 1.9 fusion.24
  147.2 1.9 fusion.24
  150.7 1.9 fusion.24
  152.9 1.1 fusion.28
  154.1 1.9 fusion.24
  156.4 1.1 fusion.28
  157.6 1.9 fusion.24
  159.8 1.1 fusion.28
  161.1 1.9 fusion.24
  163.3 1.1 fusion.28
  164.5 1.9 fusion.24
  166.8 1.1 fusion.28
  168.0 1.9 fusion.24
  170.2 1.1 fusion.28
  171.4 1.9 fusion.24
  173.7 1.1 fusion.28
  174.9 1.9 fusion.24
  178.3 1.9 fusion.24
  181.8 1.9 fusion.24
  185.2 1.9 fusion.24
  188.7 1.9 fusion.24
  192.2 1.9 fusion.24
  195.5 42.0 %pmax.7 = f32[256]{0:T(256)S(1)} all-reduce(f32[256]{0:T(256)S(1)} %get-tuple-element.42), channel_id=1, replica_groups=mesh['af'=8,'vert'=64] {'af'}, use_global_device_ids=true, to_apply=%region_5.6 | all-reduce | flops 256 | bytes 2048 | tf_op jit(solution)/shard_map/pmax | solution.py:82
  237.6 36.1 %all-reduce = (f32[3,256]{1,0:T(4,128)S(1)}, f32[256]{0:T(256)S(1)}) all-reduce(f32[3,256]{1,0:T(4,128)S(1)} %broadcast_multiply_fusion, f32[256]{0:T(256)S(1)} %get-tuple-element.93), channel_id=1, replica_groups=mesh['af'=8,'vert'=64] {'af'}, use_global_device_ids=true, to_apply=%region_6.7 | all-reduce | flops 1024 | bytes 8192 | tf_op jit(solution)/shard_map/psum | solution.py:84
  (103 shorter events, 18.3 us)
Async XLA Ops:
  7.2 18.1 %copy-start = (bf16[125,256]{1,0:T(8,128)(2,1)S(1)}, bf16[125,256]{1,0:T(8,128)(2,1)}, u32[]{:S(2)}) copy-start(bf16[125,256]{1,0:T(8,128)(2,1)} %param.6) | copy-start | bytes 192004
  7.2 130.1 %all-gather.2.cloned.1.call-start = ((), (), s32[]{:S(2)}) async-start(), calls=%async_computation.1 | async-start | bytes 2129920 | tf_op jit(solution)/shard_map/all_gather | solution.py:80
  9.5 130.7 %all-to-all-start = ((f32[64,3,512]{2,1,0:T(4,128)}), f32[64,3,512]{2,1,0:T(4,128)S(1)}, u32[]{:S(2)}, u32[]{:S(2)}) async-start(f32[64,3,512]{2,1,0:T(4,128)} %stack.2), calls=%async_computation | async-start | bytes 1048576 | tf_op jit(solution)/shard_map/all_to_all | solution.py:13
  195.5 78.7 %copy-start.1 = (f32[10,256]{1,0:T(8,128)}, f32[10,256]{1,0:T(8,128)S(1)}, u32[]{:S(2)}) copy-start(f32[10,256]{1,0:T(8,128)S(1)} %get-tuple-element.178) | copy-start | bytes 30724
Sparse Core Ops, SparseCore 0:
  10.2 127.0 all-gather.1
